TPU v7x, 32 devices: a whole 2x2x4 slice. The times are simulated.
32 devices in a mesh: groups: 2 (over x), ctx: 16 (over z, y, core).
Axes of the slice: x: 2, y: 2, z: 4, core: 2. Of those that a mesh axis runs over, the one named last changes fastest.
Arguments:
- src_cache: bfloat16 [1024, 2, 2, 16, 1024], P(('groups', 'ctx')), parts along dimension 0, may hold values from -6 to 6
- src_blocks: int32 [1024], P('groups'), parts along dimension 0, may hold values from 0 to 511, as said below
- dst_blocks: int32 [1024], P('groups'), parts along dimension 0, may hold values from 0 to 511, as said below
- ctx_lengths: int32 [8], P('groups'), parts along dimension 0, may hold values from 1024 to 2048, as said below
- queries: bfloat16 [5, 2, 8, 16384], P(None, None, 'groups'), parts along dimension 2, may hold values from -120 to 120
- new_keys: bfloat16 [5, 2, 8, 1024], P(None, None, 'groups'), parts along dimension 2, may hold values from -16 to 16
- new_values: bfloat16 [5, 2, 8, 1024], P(None, None, 'groups'), parts along dimension 2, may hold values from -6 to 6
Outputs:
- dst_cache: bfloat16 [1024, 2, 2, 16, 1024], P(('groups', 'ctx')), parts along dimension 0
- attn_out: float32 [5, 2, 1024, 128], P(None, None, ('groups', 'ctx')), parts along dimension 2
There are 2 independent parts, one for each index of `groups`. A program takes and returns all parts, laid end to end along the dimension named above; each array names one. Nothing has to cross between parts.
Inputs may be any that keep to these rules, and one draw needn't show every extreme that they name: `src_blocks`: A permutation of the blocks; device k of ctx holds source slots k * 32 to (k + 1) * 32 - 1. `dst_blocks`: A permutation of the blocks; device k of ctx holds destination slots k * 32 to (k + 1) * 32 - 1. At most 2 blocks goes from the source slots of one device to the destination slots of one device, and some pair of devices has exactly 2. `ctx_lengths`: some request has exactly 2048 cached tokens.
All inputs are finite; a program needn't handle non-finite values.
Results may differ from a plain program's by a relative error of at most 0.001.
Values may be sent and summed in bfloat16 or wider, within the bound.
No kernel may reach another device: no remote copies, remote signals or barrier semaphores. Data moves between devices by JAX's collectives and lax.ppermute only.
A program may use at most 256 MiB of HBM per device.

v0:
```python
import jax
import jax.numpy as jnp
from jax import lax
from jax.sharding import PartitionSpec as P

KVH = 8
HD = 128
QPG = 16
REQS = 4
STEPS = 4


neg_big = -1e30


def joined(value, axis, join):
    pieces = jax.tree.map(lambda part: lax.all_gather(part, axis), value)
    head = jax.tree.map(lambda part: part[0], pieces)
    tail = jax.tree.map(lambda part: part[1:], pieces)
    so_far, _ = lax.scan(lambda so_far, piece: (join(so_far, piece), None), head, tail)
    return so_far


def join_partials(earlier_part, later_part):
    max_early, total_early, sums_early = earlier_part
    max_late, total_late, sums_late = later_part
    joined_max = jnp.maximum(max_early, max_late)
    factor_early = jnp.exp(max_early - joined_max)
    factor_late = jnp.exp(max_late - joined_max)
    joined_total = total_early * factor_early + total_late * factor_late
    joined_sums = sums_early * factor_early[..., None] + sums_late * factor_late[..., None]
    return (joined_max, joined_total, joined_sums)


def migrate(src_cache, src_blocks, dst_blocks):
    devices = lax.axis_size("ctx")
    own_index = lax.axis_index("ctx")
    per_dev = src_cache.shape[0]
    block_total = src_blocks.shape[0]
    capacity = (per_dev + devices - 1) // devices
    slot_ids = jnp.arange(block_total, dtype=jnp.int32)
    inv_src = jnp.zeros((block_total,), jnp.int32).at[src_blocks].set(slot_ids)
    inv_dst = jnp.zeros((block_total,), jnp.int32).at[dst_blocks].set(slot_ids)
    target = (inv_dst[src_blocks] // per_dev).reshape(devices, per_dev)
    local_pos = jnp.arange(per_dev, dtype=jnp.int32)
    earlier = local_pos[:, None] > local_pos[None, :]
    matching = target[:, :, None] == target[:, None, :]
    bucket_rank = jnp.sum((matching & earlier[None]).astype(jnp.int32), axis=2)
    own_target = lax.dynamic_index_in_dim(target, own_index, 0, keepdims=False)
    own_rank = lax.dynamic_index_in_dim(bucket_rank, own_index, 0, keepdims=False)
    bucket = own_target * capacity + own_rank
    chosen = jnp.zeros((devices * capacity,), jnp.int32).at[bucket].set(local_pos)
    filled = jnp.zeros((devices * capacity,), jnp.int32).at[bucket].set(1) > 0
    outgoing = jnp.where(
        filled[:, None, None, None, None],
        jnp.take(src_cache, chosen, axis=0),
        jnp.zeros((), src_cache.dtype),
    )
    own_blocks = lax.dynamic_slice_in_dim(dst_blocks, own_index * per_dev, per_dev)
    root = inv_src[own_blocks]
    take_rows = root // per_dev * capacity + bucket_rank.reshape(-1)[root]
    arrived = lax.all_to_all(outgoing, "ctx", split_axis=0, concat_axis=0, tiled=True)
    return jnp.take(arrived, take_rows, axis=0)


def attend(kv_cache, block_ids, ctx_lengths, step_queries, fresh_keys, fresh_values, per_request):
    blocks, layers, _, block_len, _ = kv_cache.shape
    requests = step_queries.shape[1]
    head_rows = requests * KVH * QPG
    fresh_count = fresh_keys.shape[0]
    score_scale = HD ** (-0.5)
    highest = lax.Precision.HIGHEST
    owners = block_ids // per_request
    member = owners[:, None] == jnp.arange(requests, dtype=jnp.int32)[None, :]
    member_bf = member.astype(jnp.bfloat16)
    member_f = member.astype(jnp.float32)
    picked = jnp.einsum(
        "br,lrx->blx", member_bf, step_queries, preferred_element_type=jnp.float32
    ).astype(jnp.bfloat16)
    picked = picked.reshape(blocks, layers, KVH, QPG, HD)
    key_part = kv_cache[:, :, 0].reshape(blocks, layers, block_len, KVH, HD)
    value_part = kv_cache[:, :, 1].reshape(blocks, layers, block_len, KVH, HD)
    scores = (
        jnp.einsum("blkgd,bltkd->blkgt", picked, key_part, preferred_element_type=jnp.float32)
        * score_scale
    )
    limits = jnp.sum(jnp.where(member, ctx_lengths[None, :], 0), axis=1)
    positions = (block_ids % per_request)[:, None] * block_len + jnp.arange(
        block_len, dtype=jnp.int32
    )[None, :]
    live = (positions < limits[:, None])[:, None, None, None, :]
    scores = jnp.where(live, scores, neg_big)
    block_max = jnp.max(scores, axis=-1)
    local_max = jnp.max(
        jnp.where(member[:, :, None, None, None], block_max[:, None], neg_big), axis=0
    )
    local_max = jnp.transpose(local_max, (1, 0, 2, 3)).reshape(layers, head_rows)
    query_heads = step_queries.reshape(layers, requests, KVH, QPG, HD)
    new_key_heads = fresh_keys.reshape(fresh_count, layers, requests, KVH, HD)
    new_value_heads = fresh_values.reshape(fresh_count, layers, requests, KVH, HD).astype(
        jnp.float32
    )
    fresh_scores = (
        jnp.einsum(
            "lrkgd,slrkd->lrkgs", query_heads, new_key_heads, preferred_element_type=jnp.float32
        )
        * score_scale
    )
    fresh_max = jnp.max(fresh_scores, axis=-1).reshape(layers, head_rows)
    devices = lax.axis_size("ctx")
    share = head_rows // devices
    start = lax.axis_index("ctx") * share
    grouped = local_max.reshape(layers, requests, KVH, QPG)
    per_block = jnp.sum(jnp.where(member[:, None, :, None, None], grouped[None], 0.0), axis=2)
    weights = jnp.where(live, jnp.exp(scores - per_block[..., None]), 0.0)
    totals = jnp.einsum("br,blkg->lrkg", member_f, jnp.sum(weights, axis=-1), precision=highest)
    weighted = jnp.einsum(
        "blkgt,bltkd->blkgd", weights, value_part.astype(jnp.float32), precision=highest
    )
    weighted = jnp.einsum("br,blkgd->lrkgd", member_f, weighted, precision=highest)
    cache_totals = totals.reshape(layers, head_rows)
    cache_sums = weighted.reshape(layers, head_rows, HD)
    merged = joined((local_max, cache_totals, cache_sums), "ctx", join_partials)
    grouped = fresh_max.reshape(layers, requests, KVH, QPG)
    weights = jnp.exp(fresh_scores - grouped[..., None])
    totals = jnp.sum(weights, axis=-1).reshape(layers, head_rows)
    weighted = jnp.einsum("lrkgs,slrkd->lrkgd", weights, new_value_heads, precision=highest)
    fresh_totals = totals
    fresh_sums = weighted.reshape(layers, head_rows, HD)
    _, totals, weighted = join_partials(merged, (fresh_max, fresh_totals, fresh_sums))
    totals = lax.dynamic_slice_in_dim(totals, start, share, 1)
    weighted = lax.dynamic_slice_in_dim(weighted, start, share, 1)
    return weighted / totals[..., None]


def local(src_cache, src_blocks, dst_blocks, ctx_lengths, queries, new_keys, new_values):
    per_dev = src_cache.shape[0]
    per_request = src_blocks.shape[0] // REQS
    own_index = lax.axis_index("ctx")
    src_ids = lax.dynamic_slice_in_dim(src_blocks, own_index * per_dev, per_dev)
    dst_ids = lax.dynamic_slice_in_dim(dst_blocks, own_index * per_dev, per_dev)
    dst_cache = migrate(src_cache, src_blocks, dst_blocks)
    results = [
        attend(
            src_cache, src_ids, ctx_lengths, queries[0], new_keys[:1], new_values[:1], per_request
        )
    ]
    held_cache, held_ids = (dst_cache, dst_ids)
    for step_idx in range(1, STEPS + 1):
        results.append(
            attend(
                held_cache,
                held_ids,
                ctx_lengths,
                queries[step_idx],
                new_keys[: step_idx + 1],
                new_values[: step_idx + 1],
                per_request,
            )
        )
    return (dst_cache, jnp.stack(results))


def solution(mesh):
    in_specs = (
        P(("groups", "ctx"), None, None, None, None),
        P("groups"),
        P("groups"),
        P("groups"),
        P(None, None, "groups", None),
        P(None, None, "groups", None),
        P(None, None, "groups", None),
    )
    out_specs = (
        P(("groups", "ctx"), None, None, None, None),
        P(None, None, ("groups", "ctx"), None),
    )
    return jax.shard_map(local, mesh=mesh, in_specs=in_specs, out_specs=out_specs, check_vma=False)
```

profile of v0, /device:TPU:0, one launch (start us, length us, event | category | flops | bytes accessed | tf_op | source)
XLA Modules:
  0.0 720.0 jit_solution(13241012127152462529)
XLA Ops:
  54.7 7.7 %all-to-all-start = ((bf16[32,2,2,16,1024]{4,3,2,1,0:T(8,128)(2,1)}), bf16[32,2,2,16,1024]{4,3,2,1,0:T(8,128)(2,1)}, u32[]{:S(2)}, u32[]{:S(2)}) async-start(bf16[32,2,2,16,1024]{4,3,2,1,0:T(8,128)(2,1)} %select_select_fusion), calls=%async_computation | async-start | bytes 8388608 | tf_op jit(solution)/shard_map/all_to_all | solution.py:62
  70.8 104.9 %all-to-all-done = bf16[32,2,2,16,1024]{4,3,2,1,0:T(8,128)(2,1)} async-done(((bf16[32,2,2,16,1024]{4,3,2,1,0:T(8,128)(2,1)}), bf16[32,2,2,16,1024]{4,3,2,1,0:T(8,128)(2,1)}, u32[]{:S(2)}, u32[]{:S(2)}) %all-to-all-start) | async-done | bytes 4194336 | tf_op jit(solution)/shard_map/all_to_all | solution.py:62
  189.3 14.4 %fusion.29 = (f32[32,2,8,16]{3,2,1,0:T(8,128)S(1)}, f32[32,2,8,16]{3,2,1,0:T(8,128)S(1)}, f32[32,2,8,16,16]{3,4,2,1,0:T(8,128)}) fusion(pred[32,16]{1,0:T(8,128)(4,1)S(1)} %add_compare_fusion, f32[32,2,8,16,16]{3,4,2,1,0:T(8,128)S(1)} %fusion.46, bf16[32,2,16,8,128]{4,3,2,1,0:T(8,128)(2,1)S(1)} %bitcast.365, bf16[32,2,8,16,128]{4,3,2,0,1:T(8,128)(2,1)S(1)} %bitcast.380), kind=kOutput, calls=%fused_computation.80 | convolution fusion | flops 34324480 | bytes 5308928 | tf_op jit(solution)/shard_map/blkgd,bltkd->blkgt/dot_general | solution.py:84
  228.9 14.4 %fusion.39 = (f32[32,2,8,16]{3,2,1,0:T(8,128)}, f32[32,2,8,16]{3,2,1,0:T(8,128)}, f32[32,2,8,16]{3,2,1,0:T(8,128)}, f32[32,2,8,16]{3,2,1,0:T(8,128)}, f32[32,2,8,16,16]{3,4,2,1,0:T(8,128)}) fusion(f32[32,2,8,16,16]{3,4,2,1,0:T(8,128)} %get-tuple-element.369, f32[32,2,8,16]{3,2,1,0:T(8,128)S(1)} %copy-done.11, pred[32,16]{1,0:T(8,128)(4,1)S(1)} %add_compare_fusion, ...), kind=kOutput, calls=%fused_computation.90 | convolution fusion | flops 35618816 | bytes 6488576 | tf_op jit(solution)/shard_map/blkgd,bltkd->blkgt/dot_general | solution.py:84
  287.1 36.5 %all_gather.45 = f32[16,2,512]{2,1,0:T(2,128)S(1)} all-gather(f32[1,2,512]{2,1,0:T(2,128)} %all_gather_reshape.45), channel_id=1, replica_groups=mesh['groups'=2,'ctx'=16] {'ctx'}, dimensions={0}, use_global_device_ids=true | all-gather | bytes 69632 | tf_op jit(solution)/shard_map/all_gather | solution.py:17
  324.2 18.6 %all_gather.46 = f32[16,2,512]{2,1,0:T(2,128)S(1)} all-gather(f32[1,2,512]{2,1,0:T(2,128)} %all_gather_reshape.46), channel_id=1, replica_groups=mesh['groups'=2,'ctx'=16] {'ctx'}, dimensions={0}, use_global_device_ids=true | all-gather | bytes 69632 | tf_op jit(solution)/shard_map/all_gather | solution.py:17
  378.0 19.0 %all_gather.48 = f32[16,2,512]{2,1,0:T(2,128)S(1)} all-gather(f32[1,2,512]{2,1,0:T(2,128)S(1)} %all_gather_reshape.48), channel_id=1, replica_groups=mesh['groups'=2,'ctx'=16] {'ctx'}, dimensions={0}, use_global_device_ids=true | all-gather | bytes 69632 | tf_op jit(solution)/shard_map/all_gather | solution.py:17
  397.0 18.4 %all_gather.49 = f32[16,2,512]{2,1,0:T(2,128)S(1)} all-gather(f32[1,2,512]{2,1,0:T(2,128)S(1)} %all_gather_reshape.49), channel_id=1, replica_groups=mesh['groups'=2,'ctx'=16] {'ctx'}, dimensions={0}, use_global_device_ids=true | all-gather | bytes 69632 | tf_op jit(solution)/shard_map/all_gather | solution.py:17
  422.8 19.7 %all_gather.51 = f32[16,2,512]{2,1,0:T(2,128)S(1)} all-gather(f32[1,2,512]{2,1,0:T(2,128)S(1)} %all_gather_reshape.51), channel_id=1, replica_groups=mesh['groups'=2,'ctx'=16] {'ctx'}, dimensions={0}, use_global_device_ids=true | all-gather | bytes 69632 | tf_op jit(solution)/shard_map/all_gather | solution.py:17
  442.5 18.4 %all_gather.52 = f32[16,2,512]{2,1,0:T(2,128)S(1)} all-gather(f32[1,2,512]{2,1,0:T(2,128)S(1)} %all_gather_reshape.52), channel_id=1, replica_groups=mesh['groups'=2,'ctx'=16] {'ctx'}, dimensions={0}, use_global_device_ids=true | all-gather | bytes 69632 | tf_op jit(solution)/shard_map/all_gather | solution.py:17
  461.3 18.7 %all_gather.54 = f32[16,2,512]{2,1,0:T(2,128)S(1)} all-gather(f32[1,2,512]{2,1,0:T(2,128)S(1)} %all_gather_reshape.54), channel_id=1, replica_groups=mesh['groups'=2,'ctx'=16] {'ctx'}, dimensions={0}, use_global_device_ids=true | all-gather | bytes 69632 | tf_op jit(solution)/shard_map/all_gather | solution.py:17
  480.0 18.1 %all_gather.55 = f32[16,2,512]{2,1,0:T(2,128)S(1)} all-gather(f32[1,2,512]{2,1,0:T(2,128)S(1)} %all_gather_reshape.55), channel_id=1, replica_groups=mesh['groups'=2,'ctx'=16] {'ctx'}, dimensions={0}, use_global_device_ids=true | all-gather | bytes 69632 | tf_op jit(solution)/shard_map/all_gather | solution.py:17
  509.2 18.6 %all_gather.57 = f32[16,2,512]{2,1,0:T(2,128)S(1)} all-gather(f32[1,2,512]{2,1,0:T(2,128)S(1)} %all_gather_reshape.57), channel_id=1, replica_groups=mesh['groups'=2,'ctx'=16] {'ctx'}, dimensions={0}, use_global_device_ids=true | all-gather | bytes 69632 | tf_op jit(solution)/shard_map/all_gather | solution.py:17
  527.9 18.1 %all_gather.58 = f32[16,2,512]{2,1,0:T(2,128)S(1)} all-gather(f32[1,2,512]{2,1,0:T(2,128)S(1)} %all_gather_reshape.58), channel_id=1, replica_groups=mesh['groups'=2,'ctx'=16] {'ctx'}, dimensions={0}, use_global_device_ids=true | all-gather | bytes 69632 | tf_op jit(solution)/shard_map/all_gather | solution.py:17
  547.3 7.1 slice.209
  554.5 23.3 %while.70 = (s32[]{:T(128)}, f32[2,512]{1,0:T(2,128)S(1)}, f32[2,512]{1,0:T(2,128)S(1)}, f32[2,512,128]{2,1,0:T(8,128)S(1)}, f32[15,2,512]{2,1,0:T(2,128)S(1)}, ...) while((s32[]{:T(128)}, f32[2,512]{1,0:T(2,128)S(1)}, f32[2,512]{1,0:T(2,128)S(1)}, ...), condition=%wide.region_11.13_spmd, body=%wide.region_10.12_spmd.sunk | while | flops 399362 | bytes 1613925 | solution.py:20
  580.5 7.1 slice.217
  587.7 23.5 %while.71 = (s32[]{:T(128)}, f32[2,512]{1,0:T(2,128)S(1)}, f32[2,512]{1,0:T(2,128)S(1)}, f32[2,512,128]{2,1,0:T(8,128)S(1)}, f32[15,2,512]{2,1,0:T(2,128)S(1)}, ...) while((s32[]{:T(128)}, f32[2,512]{1,0:T(2,128)S(1)}, f32[2,512]{1,0:T(2,128)S(1)}, ...), condition=%wide.region_18.20_spmd, body=%wide.region_17.19_spmd.sunk | while | flops 399362 | bytes 1613925 | solution.py:20
  611.2 7.2 slice.223
  618.4 7.2 slice.229
  627.7 23.3 %while.72 = (s32[]{:T(128)}, f32[2,512]{1,0:T(2,128)S(1)}, f32[2,512]{1,0:T(2,128)S(1)}, f32[2,512,128]{2,1,0:T(8,128)S(1)}, f32[15,2,512]{2,1,0:T(2,128)S(1)}, ...) while((s32[]{:T(128)}, f32[2,512]{1,0:T(2,128)S(1)}, f32[2,512]{1,0:T(2,128)S(1)}, ...), condition=%wide.region_26.28_spmd, body=%wide.region_25.27_spmd.sunk | while | flops 399362 | bytes 1613925 | solution.py:20
  651.1 23.3 %while.73 = (s32[]{:T(128)}, f32[2,512]{1,0:T(2,128)S(1)}, f32[2,512]{1,0:T(2,128)S(1)}, f32[2,512,128]{2,1,0:T(8,128)S(1)}, f32[15,2,512]{2,1,0:T(2,128)S(1)}, ...) while((s32[]{:T(128)}, f32[2,512]{1,0:T(2,128)S(1)}, f32[2,512]{1,0:T(2,128)S(1)}, ...), condition=%wide.region_34.36_spmd, body=%wide.region_33.35_spmd.sunk | while | flops 399362 | bytes 1613925 | solution.py:20
  675.5 7.2 slice.235
  682.7 23.3 %while.74 = (s32[]{:T(128)}, f32[2,512]{1,0:T(2,128)S(1)}, f32[2,512]{1,0:T(2,128)S(1)}, f32[2,512,128]{2,1,0:T(8,128)S(1)}, f32[15,2,512]{2,1,0:T(2,128)S(1)}, ...) while((s32[]{:T(128)}, f32[2,512]{1,0:T(2,128)S(1)}, f32[2,512]{1,0:T(2,128)S(1)}, ...), condition=%wide.region_42.44_spmd, body=%wide.region_41.43_spmd.sunk | while | flops 399362 | bytes 1613925 | solution.py:20
  (530 shorter events, 321.7 us)
Async XLA Ops:
  7.2 539.0 %all-gather.6.cloned.1.call-start = ((), (), s32[]{:S(2)}) async-start(), calls=%async_computation.1 | async-start | bytes 8912896 | tf_op jit(solution)/shard_map/all_gather | solution.py:17
  14.0 254.8 %copy-start.51 = (s32[32]{0:T(128)}, s32[32]{0:T(128)S(1)}, u32[]{:S(2)}) copy-start(s32[32]{0:T(128)S(1)} %get-tuple-element.363) | copy-start | bytes 388
  54.7 121.0 %all-to-all-start = ((bf16[32,2,2,16,1024]{4,3,2,1,0:T(8,128)(2,1)}), bf16[32,2,2,16,1024]{4,3,2,1,0:T(8,128)(2,1)}, u32[]{:S(2)}, u32[]{:S(2)}) async-start(bf16[32,2,2,16,1024]{4,3,2,1,0:T(8,128)(2,1)} %select_select_fusion), calls=%async_computation | async-start | bytes 8388608 | tf_op jit(solution)/shard_map/all_to_all | solution.py:62
  62.5 517.0 %all-gather.8.cloned.1.call-start = ((), (), s32[]{:S(2)}) async-start(), calls=%async_computation.2 | async-start | bytes 8912896 | tf_op jit(solution)/shard_map/all_gather | solution.py:17
  70.7 133.4 %copy-start.62 = (pred[32,4]{0,1:T(4,128)(4,1)}, pred[32,4]{0,1:T(4,128)(4,1)S(1)}, u32[]{:S(2)}) copy-start(pred[32,4]{0,1:T(4,128)(4,1)S(1)} %iota_compare_fusion.1) | copy-start | bytes 388
  70.8 191.6 %copy-start.49 = (pred[32,16]{1,0:T(8,128)(4,1)}, pred[32,16]{1,0:T(8,128)(4,1)S(1)}, u32[]{:S(2)}) copy-start(pred[32,16]{1,0:T(8,128)(4,1)S(1)} %add_compare_fusion) | copy-start | bytes 1540
  218.9 392.3 %all-gather.10.cloned.1.call-start = ((), (), s32[]{:S(2)}) async-start(), calls=%async_computation.3 | async-start | bytes 8912896 | tf_op jit(solution)/shard_map/all_gather | solution.py:17
  261.5 356.9 %all-gather.12.cloned.1.call-start = ((), (), s32[]{:S(2)}) async-start(), calls=%async_computation.4 | async-start | bytes 8912896 | tf_op jit(solution)/shard_map/all_gather | solution.py:17
  273.5 400.8 %all-gather.14.cloned.1.call-start = ((), (), s32[]{:S(2)}) async-start(), calls=%async_computation.5 | async-start | bytes 8912896 | tf_op jit(solution)/shard_map/all_gather | solution.py:17
  278.5 73.3 %copy-start.15 = (bf16[1,2,4,16384]{3,2,1,0:T(4,128)(2,1)S(1)}, bf16[1,2,4,16384]{3,2,1,0:T(4,128)(2,1)}, u32[]{:S(2)}) copy-start(bf16[1,2,4,16384]{3,2,1,0:T(4,128)(2,1)} %get-tuple-element.347) | copy-start | bytes 786436
  278.5 74.3 %slice-start.2 = ((bf16[5,2,4,1024]{3,2,1,0:T(4,128)(2,1)}), bf16[3,2,4,1024]{3,2,1,0:T(4,128)(2,1)S(1)}, s32[]{:S(2)}) async-start(bf16[5,2,4,1024]{3,2,1,0:T(4,128)(2,1)} %param.24), calls=%async_computation.8 | async-start | bytes 98304 | tf_op jit(solution)/shard_map/slice | solution.py:156
  280.5 72.4 %slice-start.5 = ((bf16[5,2,4,1024]{3,2,1,0:T(4,128)(2,1)}), bf16[3,2,4,1024]{3,2,1,0:T(4,128)(2,1)S(1)}, s32[]{:S(2)}) async-start(bf16[5,2,4,1024]{3,2,1,0:T(4,128)(2,1)} %param.25), calls=%async_computation.11 | async-start | bytes 98304 | tf_op jit(solution)/shard_map/slice | solution.py:157
  281.8 76.0 %copy-start.14 = (bf16[1,2,4,16384]{3,2,1,0:T(4,128)(2,1)S(1)}, bf16[1,2,4,16384]{3,2,1,0:T(4,128)(2,1)}, u32[]{:S(2)}) copy-start(bf16[1,2,4,16384]{3,2,1,0:T(4,128)(2,1)} %get-tuple-element.350) | copy-start | bytes 786436
  281.8 76.9 %slice-start.3 = ((bf16[5,2,4,1024]{3,2,1,0:T(4,128)(2,1)}), bf16[4,2,4,1024]{3,2,1,0:T(4,128)(2,1)S(1)}, s32[]{:S(2)}) async-start(bf16[5,2,4,1024]{3,2,1,0:T(4,128)(2,1)} %param.24), calls=%async_computation.9 | async-start | bytes 131072 | tf_op jit(solution)/shard_map/slice | solution.py:156
  281.8 77.0 %slice-start.6 = ((bf16[5,2,4,1024]{3,2,1,0:T(4,128)(2,1)}), bf16[4,2,4,1024]{3,2,1,0:T(4,128)(2,1)S(1)}, s32[]{:S(2)}) async-start(bf16[5,2,4,1024]{3,2,1,0:T(4,128)(2,1)} %param.25), calls=%async_computation.12 | async-start | bytes 131072 | tf_op jit(solution)/shard_map/slice | solution.py:157
  281.8 80.3 %copy-start.13 = (bf16[1,2,4,16384]{3,2,1,0:T(4,128)(2,1)S(1)}, bf16[1,2,4,16384]{3,2,1,0:T(4,128)(2,1)}, u32[]{:S(2)}) copy-start(bf16[1,2,4,16384]{3,2,1,0:T(4,128)(2,1)} %get-tuple-element.346) | copy-start | bytes 786436
  286.1 76.3 %copy-start.19 = (bf16[5,2,4,8,128]{4,3,2,1,0:T(8,128)(2,1)S(1)}, bf16[5,2,4,8,128]{4,3,2,1,0:T(8,128)(2,1)}, u32[]{:S(2)}) copy-start(bf16[5,2,4,8,128]{4,3,2,1,0:T(8,128)(2,1)} %reshape.448) | copy-start | bytes 245764
  397.0 149.0 %copy-start.38 = (f32[16,2,512]{2,1,0:T(2,128)}, f32[16,2,512]{2,1,0:T(2,128)S(1)}, u32[]{:S(2)}) copy-start(f32[16,2,512]{2,1,0:T(2,128)S(1)} %all_gather.48) | copy-start | bytes 196612
  416.3 81.7 %copy-start.22 = (f32[4,2,8,16]{3,2,1,0:T(8,128)S(1)}, f32[4,2,8,16]{3,2,1,0:T(8,128)}, u32[]{:S(2)}) copy-start(f32[4,2,8,16]{3,2,1,0:T(8,128)} %copy-done.21) | copy-start | bytes 12292
  416.3 81.8 %copy-start.34 = (f32[32,2,8,16]{3,2,1,0:T(8,128)S(1)}, f32[32,2,8,16]{3,2,1,0:T(8,128)}, u32[]{:S(2)}) copy-start(f32[32,2,8,16]{3,2,1,0:T(8,128)} %get-tuple-element.213) | copy-start | bytes 98308
  416.3 82.2 %copy-start.12 = (f32[32,2,8,16]{3,2,1,0:T(8,128)S(1)}, f32[32,2,8,16]{3,2,1,0:T(8,128)}, u32[]{:S(2)}) copy-start(f32[32,2,8,16]{3,2,1,0:T(8,128)} %copy.331) | copy-start | bytes 98308
  416.4 82.2 %copy-start.50 = (pred[32,16]{1,0:T(8,128)(4,1)S(1)}, pred[32,16]{1,0:T(8,128)(4,1)}, u32[]{:S(2)}) copy-start(pred[32,16]{1,0:T(8,128)(4,1)} %copy-done.49) | copy-start | bytes 1540
  442.5 103.5 %copy-start.41 = (f32[16,2,512]{2,1,0:T(2,128)}, f32[16,2,512]{2,1,0:T(2,128)S(1)}, u32[]{:S(2)}) copy-start(f32[16,2,512]{2,1,0:T(2,128)S(1)} %all_gather.51) | copy-start | bytes 196612
  460.8 85.2 %copy-start.42 = (f32[16,2,512]{2,1,0:T(2,128)}, f32[16,2,512]{2,1,0:T(2,128)S(1)}, u32[]{:S(2)}) copy-start(f32[16,2,512]{2,1,0:T(2,128)S(1)} %all_gather.52) | copy-start | bytes 196612
  (70 other events, 1072.3 us)
Sparse Core Ops, SparseCore 0:
  37.1 136.3 all-gather.5
  219.0 89.8 all-gather.7
  311.1 73.2 all-gather.9
  386.4 73.9 all-gather.11
  546.3 72.7 all-gather.13
where the time goes:
time: 729 us; the launch traced here: 720 us
  blocking collectives  204 us (28%)
  other arithmetic  156 us (21%)
  local copies, waits for them, and re-layouts  125 us (17%)
  matrix products  105 us (14%)
  waiting for transfers between devices  105 us (14%)
  between operations  15.5 us (2%)
  starting transfers between devices  7.94 us (1%)
    all_gather x10, blocking collectives, joined(): pieces = jax.tree.map(lambda part: lax.all_gather(part, axis), value)  204 us
    add x75, other arithmetic, join_partials(): sums_early * factor_early[..., None] + sums_late * factor_late[..., None]  113 us
    all_to_all x1, waiting for transfers between devices, migrate(): lax.all_to_all(outgoing, 'ctx', split_axis=0, concat_axis=0, tiled=True)  105 us
    dot_general x5, matrix products, attend(): jnp.einsum('blkgd,bltkd->blkgt', picked, key_part, preferred_element_type...  37.6 us
    slice x25, local copies, waits for them, and re-layouts, joined(): tail = jax.tree.map(lambda part: part[1:], pieces)  35.8 us
    dot_general x5, matrix products, attend(): jnp.einsum('blkgt,bltkd->blkgd', weights, value_part.astype(jnp.float32),...  28.6 us
    dot_general x5, matrix products, attend(): jnp.einsum('br,blkgd->lrkgd', member_f, weighted, precision=highest)  19.3 us
    unnamed x151, local copies, waits for them, and re-layouts  18.6 us
  transfers between devices with their start and end apart: 6, of which 1 were waited for; matrix products, arithmetic and copies ran while one was open for 44% of the time, Pallas kernels for 0%

commit v1 on v0

v1 whole, which is shorter than its diff:
```python
import functools

import jax
import jax.numpy as jnp
from jax import lax
from jax.experimental import pallas as pl
from jax.experimental.pallas import tpu as pltpu
from jax.sharding import PartitionSpec as P

KVH = 8
HD = 128
LOG2E = 1.4426950408889634
NEG = -1e30
STAT = 8


def move_body(count, idx_ref, src_ref, dst_ref, sems):
    copies = [
        pltpu.make_async_copy(src_ref.at[idx_ref[c]], dst_ref.at[c], sems.at[c])
        for c in range(count)
    ]
    for copy in copies:
        copy.start()
    for copy in copies:
        copy.wait()


def move_blocks(src, idx):
    count = idx.shape[0]
    return pl.pallas_call(
        functools.partial(move_body, count),
        out_shape=jax.ShapeDtypeStruct((count,) + src.shape[1:], src.dtype),
        grid_spec=pltpu.PrefetchScalarGridSpec(
            num_scalar_prefetch=1,
            grid=(1,),
            in_specs=[pl.BlockSpec(memory_space=pl.ANY)],
            out_specs=pl.BlockSpec(memory_space=pl.ANY),
            scratch_shapes=[pltpu.SemaphoreType.DMA((count,))],
        ),
        name="move_blocks",
    )(idx, src)


def eye_mask(rows):
    return lax.broadcasted_iota(jnp.int32, (rows, HD), 0) == lax.broadcasted_iota(
        jnp.int32, (rows, HD), 1
    )


def to_lanes(value, mask):
    return jnp.sum(jnp.where(mask, value, 0.0), axis=0, keepdims=True)


def to_column(lanes, mask):
    return jnp.sum(jnp.where(mask, lanes, 0.0), axis=1, keepdims=True)


def stat_tile(max_lanes, total_lanes):
    row = lax.broadcasted_iota(jnp.int32, (STAT, HD), 0)
    return jnp.where(row == 0, max_lanes, jnp.where(row == 1, total_lanes, 0.0))


def split_dot(weights, values):
    rows = weights.shape[0]
    high = weights.astype(jnp.bfloat16)
    low = (weights - high.astype(jnp.float32)).astype(jnp.bfloat16)
    both = jnp.dot(
        jnp.concatenate([high, low], axis=0), values, preferred_element_type=jnp.float32
    )
    return both[:rows] + both[rows:]


def partial_of(query, keys, values_ones, bias, scale):
    scores = lax.dot_general(
        query, keys, (((1,), (1,)), ((), ())), preferred_element_type=jnp.float32
    )
    scores = scores * scale + bias
    top = jnp.max(scores, axis=1, keepdims=True)
    both = split_dot(jnp.exp2(scores - top), values_ones)
    return top, both[:, :HD], both[:, HD:]


def with_ones(values):
    return jnp.concatenate([values, jnp.ones_like(values)], axis=1)


def attend_body(geo, bit_ref, q_ref, k_ref, v_ref, bias_ref, send_ref, keep_ref):
    requests, layers, pieces, flats, rows, scale = geo
    layer, head = pl.program_id(0), pl.program_id(1)
    tokens = k_ref.shape[0] * k_ref.shape[3]
    keys = k_ref[:, 0, 0].reshape(tokens, HD)
    values = with_ones(v_ref[:, 0, 0].reshape(tokens, HD))
    mask = eye_mask(rows)
    heads = pl.num_programs(1)
    for req in range(requests):
        query = q_ref[0, 0, req * pieces * rows:(req + 1) * pieces * rows]
        top, sums, totals = partial_of(query, keys, values, bias_ref[req:req + 1], scale)
        for piece in range(pieces):
            part = slice(piece * rows, (piece + 1) * rows)
            tile = stat_tile(to_lanes(top[part], mask), to_lanes(totals[part], mask))
            flat = (req * heads + head) * pieces + piece
            share = flat // flats
            chunk = (flat % flats) * layers + layer
            out_sums = sums[part]

            def put(ref):
                ref[share // 2, chunk, :rows, :] = out_sums
                ref[share // 2, chunk, rows:, :] = tile

            pl.when(share % 2 == bit_ref[0])(functools.partial(put, keep_ref))
            pl.when(share % 2 != bit_ref[0])(functools.partial(put, send_ref))


def merge(first, second, rows, mask):
    max_a, max_b = first[rows:rows + 1], second[rows:rows + 1]
    top = jnp.maximum(max_a, max_b)
    fac_a, fac_b = jnp.exp2(max_a - top), jnp.exp2(max_b - top)
    total = first[rows + 1:rows + 2] * fac_a + second[rows + 1:rows + 2] * fac_b
    sums = first[:rows] * to_column(fac_a, mask) + second[:rows] * to_column(fac_b, mask)
    return sums, top, total


def merge_body(rows, bit_ref, have_ref, came_ref, send_ref, keep_ref):
    mask = eye_mask(rows)
    half, chunks = send_ref.shape[0], send_ref.shape[1]

    for choice, out_ref in ((1 - bit_ref[0], send_ref), (bit_ref[0], keep_ref)):

        def step(i, carry, choice=choice, out_ref=out_ref):
            share, chunk = i // chunks, i % chunks
            where = 2 * share + choice
            sums, top, total = merge(have_ref[where, chunk], came_ref[where, chunk], rows, mask)
            out_ref[share, chunk, :rows, :] = sums
            out_ref[share, chunk, rows:, :] = stat_tile(top, total)
            return carry

        lax.fori_loop(0, half * chunks, step, 0)


def merge_halves(have, came, bit, rows):
    shape = jax.ShapeDtypeStruct((have.shape[0] // 2,) + have.shape[1:], have.dtype)
    full = pl.BlockSpec(have.shape, lambda i, b: (0, 0, 0, 0))
    part = pl.BlockSpec(shape.shape, lambda i, b: (0, 0, 0, 0))
    return pl.pallas_call(
        functools.partial(merge_body, rows),
        out_shape=(shape, shape),
        grid_spec=pltpu.PrefetchScalarGridSpec(
            num_scalar_prefetch=1, grid=(1,), in_specs=[full, full], out_specs=(part, part)
        ),
        name="merge_halves",
    )(bit, have, came)


def fresh_body(geo, q_ref, k_ref, v_ref, out_ref):
    rows, group, fresh, scale = geo
    mask = eye_mask(rows)
    chunks, width = k_ref.shape[0], k_ref.shape[1]
    step = lax.broadcasted_iota(jnp.int32, (rows, width), 0) // group
    token = lax.broadcasted_iota(jnp.int32, (rows, width), 1)
    bias = jnp.where((token <= step) & (token < fresh), 0.0, NEG)
    for chunk in range(chunks):
        top, sums, totals = partial_of(
            q_ref[chunk], k_ref[chunk], with_ones(v_ref[chunk]), bias, scale
        )
        out_ref[chunk, :rows, :] = sums
        out_ref[chunk, rows:, :] = stat_tile(to_lanes(top, mask), to_lanes(totals, mask))


def final_body(geo, have_ref, came_ref, fresh_ref, out_ref):
    rows, group, layers = geo
    mask = eye_mask(rows)
    for chunk in range(fresh_ref.shape[0]):
        sums, top, total = merge(have_ref[0, chunk], came_ref[0, chunk], rows, mask)
        both = jnp.concatenate([sums, stat_tile(top, total)], axis=0)
        sums, _, total = merge(both, fresh_ref[chunk], rows, mask)
        lane = lax.broadcasted_iota(jnp.int32, (1, HD), 1)
        total = jnp.where(lane < rows, total, 1.0)
        result = sums * to_column(1.0 / total, mask)
        flat, layer = chunk // layers, chunk % layers
        for step in range(rows // group):
            out_ref[step, layer, flat * group:(flat + 1) * group, :] = result[
                step * group:(step + 1) * group
            ]


def local(src_cache, src_blocks, dst_blocks, ctx_lengths, queries, new_keys, new_values):
    devices = lax.axis_size("ctx")
    me = lax.axis_index("ctx")
    per_dev, layers, _, block_len, _ = src_cache.shape
    block_total = src_blocks.shape[0]
    steps, _, requests, width = queries.shape
    group_all = width // (KVH * HD)
    per_request = block_total // requests
    capacity = (per_dev + devices - 1) // devices
    slot_ids = jnp.arange(block_total, dtype=jnp.int32)
    own_slots = jnp.arange(per_dev, dtype=jnp.int32)
    i32 = lambda flags: flags.astype(jnp.int32)

    own_src = lax.dynamic_slice_in_dim(src_blocks, me * per_dev, per_dev)
    own_dst = lax.dynamic_slice_in_dim(dst_blocks, me * per_dev, per_dev)
    goes_to = jnp.sum(i32(own_src[:, None] == dst_blocks[None, :]) * slot_ids[None, :], axis=1)
    target = goes_to // per_dev
    earlier = own_slots[None, :] < own_slots[:, None]
    rank = jnp.sum(i32((target[:, None] == target[None, :]) & earlier), axis=1)
    bucket = target * capacity + rank
    buckets = jnp.arange(devices * capacity, dtype=jnp.int32)
    chosen = jnp.sum(i32(buckets[:, None] == bucket[None, :]) * own_slots[None, :], axis=1)
    root = jnp.sum(i32(own_dst[:, None] == src_blocks[None, :]) * slot_ids[None, :], axis=1)
    origin = root // per_dev
    before = (origin[:, None] == origin[None, :]) & (root[None, :] < root[:, None])
    take_rows = origin * capacity + jnp.sum(i32(before), axis=1)

    outgoing = move_blocks(src_cache, chosen)
    arrived = lax.all_to_all(outgoing, "ctx", split_axis=0, concat_axis=0, tiled=True)

    pieces = max(1, devices // (requests * KVH))
    group = group_all // pieces
    flats = requests * KVH * pieces // devices
    rows = steps * group
    chunks = flats * layers
    scale = HD ** -0.5 * LOG2E
    query_rows = queries.reshape(steps, layers, requests, KVH, pieces, group, HD)
    query_rows = jnp.transpose(query_rows, (1, 3, 2, 4, 0, 5, 6))
    query_rows = query_rows.reshape(layers, KVH, requests * pieces * rows, HD)
    positions = (own_src % per_request)[:, None] * block_len + jnp.arange(
        block_len, dtype=jnp.int32
    )
    request_ids = jnp.arange(requests, dtype=jnp.int32)
    live = ((own_src // per_request)[None, :, None] == request_ids[:, None, None]) & (
        positions[None] < ctx_lengths[:, None, None]
    )
    bias = jnp.where(live, 0.0, NEG).astype(jnp.float32).reshape(requests, per_dev * block_len)
    bits = devices.bit_length() - 1
    bit_of = [((me >> b) & 1).astype(jnp.int32).reshape(1) for b in range(bits)]
    half = jax.ShapeDtypeStruct((devices // 2, chunks, rows + STAT, HD), jnp.float32)
    cache_block = (per_dev, 1, 1, block_len, HD)
    resident = pl.BlockSpec(half.shape, lambda l, k, b: (0, 0, 0, 0))
    send, keep = pl.pallas_call(
        functools.partial(attend_body, (requests, layers, pieces, flats, rows, scale)),
        out_shape=(half, half),
        grid_spec=pltpu.PrefetchScalarGridSpec(
            num_scalar_prefetch=1,
            grid=(layers, KVH),
            in_specs=[
                pl.BlockSpec((1, 1) + query_rows.shape[2:], lambda l, k, b: (l, k, 0, 0)),
                pl.BlockSpec(cache_block, lambda l, k, b: (0, l, 0, 0, k)),
                pl.BlockSpec(cache_block, lambda l, k, b: (0, l, 1, 0, k)),
                pl.BlockSpec(bias.shape, lambda l, k, b: (0, 0)),
            ],
            out_specs=(resident, resident),
        ),
        name="attend",
    )(bit_of[0], query_rows, src_cache, src_cache, bias)

    share = requests * KVH * group_all // devices
    heads = KVH * group_all
    own_req, own_head = me * share // heads, me * share % heads
    own_q = lax.dynamic_slice(
        queries, (0, 0, own_req, own_head * HD), (steps, layers, 1, share * HD)
    ).reshape(steps, layers, flats, group, HD)
    own_q = jnp.transpose(own_q, (2, 1, 0, 3, 4)).reshape(chunks, rows, HD)
    fresh_count = new_keys.shape[0]
    kv_heads = max(1, share // group_all)

    def own_fresh(tokens):
        own = lax.dynamic_slice(
            tokens,
            (0, 0, own_req, own_head // group_all * HD),
            (fresh_count, layers, 1, kv_heads * HD),
        ).reshape(fresh_count, layers, kv_heads, HD)
        own = jnp.repeat(jnp.transpose(own, (2, 1, 0, 3)), flats // kv_heads, axis=0)
        own = own.reshape(chunks, fresh_count, HD)
        return jnp.pad(own, ((0, 0), (0, -fresh_count % 16), (0, 0)))

    fresh = pl.pallas_call(
        functools.partial(fresh_body, (rows, group, fresh_count, scale)),
        out_shape=jax.ShapeDtypeStruct((chunks, rows + STAT, HD), jnp.float32),
        name="fresh",
    )(own_q, own_fresh(new_keys), own_fresh(new_values))

    for b in range(bits):
        pairs = [(i, i ^ (1 << b)) for i in range(devices)]
        came = lax.ppermute(send, "ctx", pairs)
        if b + 1 < bits:
            send, keep = merge_halves(keep, came, bit_of[b + 1], rows)
    attn_out = pl.pallas_call(
        functools.partial(final_body, (rows, group, layers)),
        out_shape=jax.ShapeDtypeStruct((steps, layers, share, HD), jnp.float32),
        name="final",
    )(keep, came, fresh)

    dst_cache = move_blocks(arrived, take_rows)
    return dst_cache, attn_out


def solution(mesh):
    in_specs = (
        P(("groups", "ctx"), None, None, None, None),
        P("groups"),
        P("groups"),
        P("groups"),
        P(None, None, "groups", None),
        P(None, None, "groups", None),
        P(None, None, "groups", None),
    )
    out_specs = (
        P(("groups", "ctx"), None, None, None, None),
        P(None, None, ("groups", "ctx"), None),
    )
    return jax.shard_map(local, mesh=mesh, in_specs=in_specs, out_specs=out_specs, check_vma=False)
```

time: 729 us -> 386 us (0.53); the launches traced: 720 us -> 385 us
  Pallas kernels: 0 us -> 310 us
  blocking collectives: 204 us -> 0 us
  other arithmetic: 156 us -> 4.1 us
  local copies, waits for them, and re-layouts: 125 us -> 9.85 us
  matrix products: 105 us -> 0 us
  waiting for transfers between devices: 105 us -> 40.1 us
  between operations: 15.5 us -> 0.78 us
  starting transfers between devices: 7.94 us -> 20.4 us
    pallas_call x0 -> x8, Pallas kernels: none -> 310 us  [the longest x2 258 us: move_blocks(): pl.pallas_call(functools.partial(move_body, count), out_shape=jax.ShapeDt...]
    all_gather x10 -> x0, blocking collectives: 204 us -> none  [joined(): pieces = jax.tree.map(lambda part: lax.all_gather(part, axis), value)]
    add x155 -> x3, other arithmetic: 119 us -> 0.6 us  [the longest x1 0.58 us: local(): take_rows = origin * capacity + jnp.sum(i32(before), axis=1)]
    dot_general x34 -> x0, matrix products: 105 us -> none  [the longest x5 37.6 us: attend(): jnp.einsum('blkgd,bltkd->blkgt', picked, key_part, preferred_element_type...]
    all_to_all x1, waiting for transfers between devices: 105 us -> 0.01 us  [local(): lax.all_to_all(outgoing, 'ctx', split_axis=0, concat_axis=0, tiled=True)]
    slice x42 -> x0, local copies, waits for them, and re-layouts: 41.9 us -> none  [the longest x25 35.8 us: joined(): tail = jax.tree.map(lambda part: part[1:], pieces)]
    ppermute x0 -> x4, waiting for transfers between devices: none -> 40.1 us  [local(): came = lax.ppermute(send, 'ctx', pairs)]
    unnamed x151 -> x12, local copies, waits for them, and re-layouts: 18.6 us -> 2.28 us
  transfers between devices with their start and end apart: 6 -> 5, of which waited for: 1 -> 4; matrix products, arithmetic and copies ran while one was open for 44% -> 2% of each run, Pallas kernels for 0% -> 13%
where the time goes in v1:
time: 386 us; the launch traced here: 385 us
  Pallas kernels  310 us (80%)
  waiting for transfers between devices  40.1 us (10%)
  starting transfers between devices  20.4 us (5%)
  local copies, waits for them, and re-layouts  9.85 us (3%)
  other arithmetic  4.1 us (1%)
    pallas_call x2, Pallas kernels, move_blocks(): pl.pallas_call(functools.partial(move_body, count), out_shape=jax.ShapeDt...  258 us
    ppermute x4, waiting for transfers between devices, local(): came = lax.ppermute(send, 'ctx', pairs)  40.1 us
    pallas_call x1, Pallas kernels, local(): pl.pallas_call(functools.partial(attend_body, (requests, layers, pieces,...  34.6 us
    ppermute x4, starting transfers between devices, local(): came = lax.ppermute(send, 'ctx', pairs)  12.8 us
    pallas_call x3, Pallas kernels, merge_halves(): pl.pallas_call(functools.partial(merge_body, rows), out_shape=(shape, sha...  12.8 us
  transfers between devices with their start and end apart: 5, of which 4 were waited for; matrix products, arithmetic and copies ran while one was open for 2% of the time, Pallas kernels for 13%

profile of v1, /device:TPU:0, one launch (start us, length us, event | category | flops | bytes accessed | tf_op | source)
XLA Modules:
  0.0 385.2 jit_solution(8101649974569708978)
XLA Ops:
  0.6 0.8 fusion.1
  1.4 0.9 select_reduce_fusion
  3.1 129.1 %move_blocks.2 = bf16[32,2,2,16,1024]{4,3,2,1,0:T(8,128)(2,1)} custom-call(s32[32]{0:T(128)} %select_reduce_fusion.2.idx_ref, bf16[32,2,2,16,1024]{4,3,2,1,0:T(8,128)(2,1)} %v_ref.1), custom_call_target="tpu_custom_call" | custom-call | tf_op jit(solution)/shard_map/move_blocks/pallas_call | solution.py:30
  132.2 7.6 %all-to-all-start = ((bf16[32,2,2,16,1024]{4,3,2,1,0:T(8,128)(2,1)}), bf16[32,2,2,16,1024]{4,3,2,1,0:T(8,128)(2,1)}, u32[]{:S(2)}, u32[]{:S(2)}) async-start(bf16[32,2,2,16,1024]{4,3,2,1,0:T(8,128)(2,1)} %move_blocks.2), calls=%async_computation | async-start | bytes 8388608 | tf_op jit(solution)/shard_map/all_to_all | solution.py:214
  139.9 1.4 reshape.163
  141.3 1.4 copy.14
  143.8 34.6 %attend.1 = (f32[8,4,88,128]{3,2,1,0:T(8,128)}, f32[8,4,88,128]{3,2,1,0:T(8,128)}) custom-call(s32[1]{0:T(128)} %bitcast.3.bit_ref, bf16[2,8,320,128]{3,2,1,0:T(8,128)(2,1)} %bitcast.15, bf16[32,2,2,16,1024]{4,3,2,1,0:T(8,128)(2,1)} %v_ref.1, bf16[32,2,2,16,1024]{4,3,2,1,0:T(8,128)(2,1)} %v_ref.1, f32[4,512]{1,0:T(4,128)} %and_select_fusion.bias_ref), custom_call_target="tpu_custom_call" | custom-call | tf_op jit(solution)/shard_map/attend/pallas_call | solution.py:238
  178.8 3.2 collective-permute-done.came_ref
  182.0 6.3 %merge_halves.3 = (f32[4,4,88,128]{3,2,1,0:T(8,128)}, f32[4,4,88,128]{3,2,1,0:T(8,128)}) custom-call(s32[1]{0:T(128)} %bitcast.2.bit_ref, f32[8,4,88,128]{3,2,1,0:T(8,128)} %get-tuple-element.10.have_ref, f32[8,4,88,128]{3,2,1,0:T(8,128)} %collective-permute-done.came_ref), custom_call_target="tpu_custom_call" | custom-call | tf_op jit(solution)/shard_map/merge_halves/pallas_call | solution.py:144
  188.3 1.9 collective-permute-start.1
  190.2 0.8 dynamic_slice.15
  191.1 26.7 %collective-permute-done.1.came_ref = f32[4,4,88,128]{3,2,1,0:T(8,128)S(1)} collective-permute-done((f32[4,4,88,128]{3,2,1,0:T(8,128)}, f32[4,4,88,128]{3,2,1,0:T(8,128)S(1)}, u32[]{:S(2)}, u32[]{:S(2)}) %collective-permute-start.1) | collective-permute-done | bytes 720928 | tf_op jit(solution)/shard_map/ppermute | solution.py:283
  217.8 0.9 copy-done.1
  218.7 3.9 %merge_halves.4 = (f32[2,4,88,128]{3,2,1,0:T(8,128)}, f32[2,4,88,128]{3,2,1,0:T(8,128)}) custom-call(s32[1]{0:T(128)} %bitcast.1.bit_ref, f32[4,4,88,128]{3,2,1,0:T(8,128)} %get-tuple-element.12.have_ref, f32[4,4,88,128]{3,2,1,0:T(8,128)} %copy-done.1), custom_call_target="tpu_custom_call" | custom-call | tf_op jit(solution)/shard_map/merge_halves/pallas_call | solution.py:144
  222.5 1.1 collective-permute-start.2
  223.6 0.8 dynamic-slice_reduce_fusion
  225.1 0.9 dynamic-slice_reduce_fusion.1
  227.3 2.2 fresh.1.fresh_ref
  229.7 2.0 collective-permute-done.2.came_ref
  232.4 2.6 merge_halves.5
  235.0 9.5 %collective-permute-start.3 = (f32[1,4,88,128]{3,2,1,0:T(8,128)}, f32[1,4,88,128]{3,2,1,0:T(8,128)S(1)}, u32[]{:S(2)}, u32[]{:S(2)}) collective-permute-start(f32[1,4,88,128]{3,2,1,0:T(8,128)} %get-tuple-element.17), channel_id=1, source_target_pairs={{0,8},{1,9},{2,10},{3,11},{4,12},{5,13},{6,14},{7,15},{8,0},{9,1},... | collective-permute-start | bytes 540680 | tf_op jit(solution)/shard_map/ppermute | solution.py:283
  245.2 8.2 %collective-permute-done.3.came_ref = f32[1,4,88,128]{3,2,1,0:T(8,128)S(1)} collective-permute-done((f32[1,4,88,128]{3,2,1,0:T(8,128)}, f32[1,4,88,128]{3,2,1,0:T(8,128)S(1)}, u32[]{:S(2)}, u32[]{:S(2)}) %collective-permute-start.3) | collective-permute-done | bytes 180256 | tf_op jit(solution)/shard_map/ppermute | solution.py:283
  254.0 2.1 final.1
  256.1 129.1 %move_blocks.3 = bf16[32,2,2,16,1024]{4,3,2,1,0:T(8,128)(2,1)} custom-call(s32[32]{0:T(128)} %multiply_add_fusion.1.idx_ref, bf16[32,2,2,16,1024]{4,3,2,1,0:T(8,128)(2,1)} %all-to-all-done.src_ref), custom_call_target="tpu_custom_call" | custom-call | tf_op jit(solution)/shard_map/move_blocks/pallas_call | solution.py:30
  (38 shorter events, 6.6 us)
Async XLA Ops:
  132.2 7.6 %copy-start = (bf16[5,2,4,16384]{3,2,1,0:T(4,128)(2,1)S(1)}, bf16[5,2,4,16384]{3,2,1,0:T(4,128)(2,1)}, u32[]{:S(2)}) copy-start(bf16[5,2,4,16384]{3,2,1,0:T(4,128)(2,1)} %param.11) | copy-start | bytes 3932164
  132.2 123.8 %all-to-all-start = ((bf16[32,2,2,16,1024]{4,3,2,1,0:T(8,128)(2,1)}), bf16[32,2,2,16,1024]{4,3,2,1,0:T(8,128)(2,1)}, u32[]{:S(2)}, u32[]{:S(2)}) async-start(bf16[32,2,2,16,1024]{4,3,2,1,0:T(8,128)(2,1)} %move_blocks.2), calls=%async_computation | async-start | bytes 8388608 | tf_op jit(solution)/shard_map/all_to_all | solution.py:214
  141.3 1.9 copy-start.5
  178.4 3.6 collective-permute-start
  182.0 8.9 %copy-start.4 = (s32[512]{0:T(512)S(1)}, s32[512]{0:T(512)}, u32[]{:S(2)}) copy-start(s32[512]{0:T(512)} %param.8) | copy-start | bytes 6148
  188.3 29.5 %collective-permute-start.1 = (f32[4,4,88,128]{3,2,1,0:T(8,128)}, f32[4,4,88,128]{3,2,1,0:T(8,128)S(1)}, u32[]{:S(2)}, u32[]{:S(2)}) collective-permute-start(f32[4,4,88,128]{3,2,1,0:T(8,128)} %get-tuple-element.13), channel_id=1, source_target_pairs={{0,2},{1,3},{2,0},{3,1},{4,6},{5,7},{6,4},{7,5},{8,10},{9,11},{10,... | collective-permute-start | bytes 2162696 | tf_op jit(solution)/shard_map/ppermute | solution.py:283
  217.8 0.9 copy-start.1
  222.5 9.2 %collective-permute-start.2 = (f32[2,4,88,128]{3,2,1,0:T(8,128)}, f32[2,4,88,128]{3,2,1,0:T(8,128)S(1)}, u32[]{:S(2)}, u32[]{:S(2)}) collective-permute-start(f32[2,4,88,128]{3,2,1,0:T(8,128)} %get-tuple-element.15), channel_id=1, source_target_pairs={{0,4},{1,5},{2,6},{3,7},{4,0},{5,1},{6,2},{7,3},{8,12},{9,13},{10,... | collective-permute-start | bytes 1081352 | tf_op jit(solution)/shard_map/ppermute | solution.py:283
  231.7 0.7 copy-start.2
  235.0 18.3 %collective-permute-start.3 = (f32[1,4,88,128]{3,2,1,0:T(8,128)}, f32[1,4,88,128]{3,2,1,0:T(8,128)S(1)}, u32[]{:S(2)}, u32[]{:S(2)}) collective-permute-start(f32[1,4,88,128]{3,2,1,0:T(8,128)} %get-tuple-element.17), channel_id=1, source_target_pairs={{0,8},{1,9},{2,10},{3,11},{4,12},{5,13},{6,14},{7,15},{8,0},{9,1},... | collective-permute-start | bytes 540680 | tf_op jit(solution)/shard_map/ppermute | solution.py:283
  253.4 0.7 copy-start.3

commit v2 on v1

--- a/solution.py
+++ b/solution.py
@@ -14,15 +14,21 @@
 STAT = 8
 
 
-def move_body(count, idx_ref, src_ref, dst_ref, sems):
-    copies = [
-        pltpu.make_async_copy(src_ref.at[idx_ref[c]], dst_ref.at[c], sems.at[c])
+def move_body(count, idx_ref, src_ref, dst_ref, held, in_sems, out_sems):
+    loads = [
+        pltpu.make_async_copy(src_ref.at[idx_ref[c]], held.at[c], in_sems.at[c])
         for c in range(count)
     ]
-    for copy in copies:
-        copy.start()
-    for copy in copies:
-        copy.wait()
+    stores = [
+        pltpu.make_async_copy(held.at[c], dst_ref.at[c], out_sems.at[c]) for c in range(count)
+    ]
+    for load in loads:
+        load.start()
+    for load, store in zip(loads, stores):
+        load.wait()
+        store.start()
+    for store in stores:
+        store.wait()
 
 
 def move_blocks(src, idx):
@@ -35,7 +41,11 @@
             grid=(1,),
             in_specs=[pl.BlockSpec(memory_space=pl.ANY)],
             out_specs=pl.BlockSpec(memory_space=pl.ANY),
-            scratch_shapes=[pltpu.SemaphoreType.DMA((count,))],
+            scratch_shapes=[
+                pltpu.VMEM((count,) + src.shape[1:], src.dtype),
+                pltpu.SemaphoreType.DMA((count,)),
+                pltpu.SemaphoreType.DMA((count,)),
+            ],
         ),
         name="move_blocks",
     )(idx, src)

time: 386 us -> 138 us (0.36)
  Pallas kernels: 310 us -> 62.1 us
    pallas_call x2, Pallas kernels: 258 us -> 10.4 us  [move_blocks(): pl.pallas_call(functools.partial(move_body, count), out_shape=jax.ShapeDt...]
  transfers between devices with their start and end apart: 5 -> 5, of which waited for: 4 -> 4; matrix products, arithmetic and copies ran while one was open for 2% -> 7% of each run, Pallas kernels for 13% -> 38%
where the time goes in v2:
time: 138 us; the launch traced here: 137 us
  Pallas kernels  62.1 us (45%)
  waiting for transfers between devices  40.1 us (29%)
  starting transfers between devices  20.4 us (15%)
  local copies, waits for them, and re-layouts  9.85 us (7%)
  other arithmetic  4.1 us (3%)
    ppermute x4, waiting for transfers between devices, local(): came = lax.ppermute(send, 'ctx', pairs)  40.1 us
    pallas_call x1, Pallas kernels, local(): pl.pallas_call(functools.partial(attend_body, (requests, layers, pieces,...  34.6 us
    ppermute x4, starting transfers between devices, local(): came = lax.ppermute(send, 'ctx', pairs)  12.8 us
    pallas_call x3, Pallas kernels, merge_halves(): pl.pallas_call(functools.partial(merge_body, rows), out_shape=(shape, sha...  12.8 us
    pallas_call x2, Pallas kernels, move_blocks(): pl.pallas_call(functools.partial(move_body, count), out_shape=jax.ShapeDt...  10.4 us
    all_to_all x1, starting transfers between devices, local(): lax.all_to_all(outgoing, 'ctx', split_axis=0, concat_axis=0, tiled=True)  7.61 us
    reshape x2, local copies, waits for them, and re-layouts, local(): queries.reshape(steps, layers, requests, KVH, pieces, group, HD)  2.78 us
  transfers between devices with their start and end apart: 5, of which 4 were waited for; matrix products, arithmetic and copies ran while one was open for 7% of the time, Pallas kernels for 38%

profile of v2, /device:TPU:0, one launch (start us, length us, event | category | flops | bytes accessed | tf_op | source)
XLA Modules:
  0.0 137.3 jit_solution(11537816607251308700)
XLA Ops:
  0.6 0.8 fusion.1
  1.4 0.9 select_reduce_fusion
  3.1 5.2 %move_blocks.2 = bf16[32,2,2,16,1024]{4,3,2,1,0:T(8,128)(2,1)} custom-call(s32[32]{0:T(128)} %select_reduce_fusion.2.idx_ref, bf16[32,2,2,16,1024]{4,3,2,1,0:T(8,128)(2,1)} %v_ref.1), custom_call_target="tpu_custom_call" | custom-call | tf_op jit(solution)/shard_map/move_blocks/pallas_call | solution.py:36
  8.3 7.6 %all-to-all-start = ((bf16[32,2,2,16,1024]{4,3,2,1,0:T(8,128)(2,1)}), bf16[32,2,2,16,1024]{4,3,2,1,0:T(8,128)(2,1)}, u32[]{:S(2)}, u32[]{:S(2)}) async-start(bf16[32,2,2,16,1024]{4,3,2,1,0:T(8,128)(2,1)} %move_blocks.2), calls=%async_computation | async-start | bytes 8388608 | tf_op jit(solution)/shard_map/all_to_all | solution.py:224
  15.9 1.4 %reshape.163 = bf16[5,2,4,8,1,16,128]{6,5,3,2,1,0,4:T(8,128)(2,1)S(1)} reshape(bf16[5,2,4,16384]{3,2,1,0:T(4,128)(2,1)S(1)} %copy-done) | data formatting | bytes 2621440 | tf_op jit(solution)/shard_map/reshape | solution.py:232
  17.3 1.4 %copy.14 = bf16[5,2,4,8,1,16,128]{6,5,0,2,3,1,4:T(8,128)(2,1)} copy(bf16[5,2,4,8,1,16,128]{6,5,3,2,1,0,4:T(8,128)(2,1)S(1)} %reshape.163) | data formatting | bytes 2621440 | tf_op jit(solution)/shard_map/reshape | solution.py:232
  19.9 34.6 %attend.1 = (f32[8,4,88,128]{3,2,1,0:T(8,128)}, f32[8,4,88,128]{3,2,1,0:T(8,128)}) custom-call(s32[1]{0:T(128)} %bitcast.3.bit_ref, bf16[2,8,320,128]{3,2,1,0:T(8,128)(2,1)} %bitcast.15, bf16[32,2,2,16,1024]{4,3,2,1,0:T(8,128)(2,1)} %v_ref.1, bf16[32,2,2,16,1024]{4,3,2,1,0:T(8,128)(2,1)} %v_ref.1, f32[4,512]{1,0:T(4,128)} %and_select_fusion.bias_ref), custom_call_target="tpu_custom_call" | custom-call | tf_op jit(solution)/shard_map/attend/pallas_call | solution.py:248
  54.9 3.2 %collective-permute-done.came_ref = f32[8,4,88,128]{3,2,1,0:T(8,128)} collective-permute-done((f32[8,4,88,128]{3,2,1,0:T(8,128)}, f32[8,4,88,128]{3,2,1,0:T(8,128)}, u32[]{:S(2)}, u32[]{:S(2)}) %collective-permute-start) | collective-permute-done | bytes 1441824 | tf_op jit(solution)/shard_map/ppermute | solution.py:293
  58.1 6.3 %merge_halves.3 = (f32[4,4,88,128]{3,2,1,0:T(8,128)}, f32[4,4,88,128]{3,2,1,0:T(8,128)}) custom-call(s32[1]{0:T(128)} %bitcast.2.bit_ref, f32[8,4,88,128]{3,2,1,0:T(8,128)} %get-tuple-element.10.have_ref, f32[8,4,88,128]{3,2,1,0:T(8,128)} %collective-permute-done.came_ref), custom_call_target="tpu_custom_call" | custom-call | tf_op jit(solution)/shard_map/merge_halves/pallas_call | solution.py:154
  64.4 1.9 %collective-permute-start.1 = (f32[4,4,88,128]{3,2,1,0:T(8,128)}, f32[4,4,88,128]{3,2,1,0:T(8,128)S(1)}, u32[]{:S(2)}, u32[]{:S(2)}) collective-permute-start(f32[4,4,88,128]{3,2,1,0:T(8,128)} %get-tuple-element.13), channel_id=1, source_target_pairs={{0,2},{1,3},{2,0},{3,1},{4,6},{5,7},{6,4},{7,5},{8,10},{9,11},{10,... | collective-permute-start | bytes 2162696 | tf_op jit(solution)/shard_map/ppermute | solution.py:293
  66.2 0.8 dynamic_slice.15
  67.2 26.7 %collective-permute-done.1.came_ref = f32[4,4,88,128]{3,2,1,0:T(8,128)S(1)} collective-permute-done((f32[4,4,88,128]{3,2,1,0:T(8,128)}, f32[4,4,88,128]{3,2,1,0:T(8,128)S(1)}, u32[]{:S(2)}, u32[]{:S(2)}) %collective-permute-start.1) | collective-permute-done | bytes 720928 | tf_op jit(solution)/shard_map/ppermute | solution.py:293
  93.9 0.9 copy-done.1
  94.7 3.9 %merge_halves.4 = (f32[2,4,88,128]{3,2,1,0:T(8,128)}, f32[2,4,88,128]{3,2,1,0:T(8,128)}) custom-call(s32[1]{0:T(128)} %bitcast.1.bit_ref, f32[4,4,88,128]{3,2,1,0:T(8,128)} %get-tuple-element.12.have_ref, f32[4,4,88,128]{3,2,1,0:T(8,128)} %copy-done.1), custom_call_target="tpu_custom_call" | custom-call | tf_op jit(solution)/shard_map/merge_halves/pallas_call | solution.py:154
  98.6 1.1 collective-permute-start.2
  99.7 0.8 dynamic-slice_reduce_fusion
  101.2 0.9 dynamic-slice_reduce_fusion.1
  103.3 2.2 %fresh.1.fresh_ref = f32[4,88,128]{2,1,0:T(8,128)} custom-call(bf16[4,80,128]{2,1,0:T(8,128)(2,1)} %bitcast.16, bf16[4,16,128]{2,1,0:T(8,128)(2,1)} %pad.7.k_ref, bf16[4,16,128]{2,1,0:T(8,128)(2,1)} %pad.8.v_ref), custom_call_target="tpu_custom_call" | custom-call | tf_op jit(solution)/shard_map/fresh/pallas_call | solution.py:285
  105.8 2.0 %collective-permute-done.2.came_ref = f32[2,4,88,128]{3,2,1,0:T(8,128)S(1)} collective-permute-done((f32[2,4,88,128]{3,2,1,0:T(8,128)}, f32[2,4,88,128]{3,2,1,0:T(8,128)S(1)}, u32[]{:S(2)}, u32[]{:S(2)}) %collective-permute-start.2) | collective-permute-done | bytes 360480 | tf_op jit(solution)/shard_map/ppermute | solution.py:293
  108.5 2.6 %merge_halves.5 = (f32[1,4,88,128]{3,2,1,0:T(8,128)}, f32[1,4,88,128]{3,2,1,0:T(8,128)}) custom-call(s32[1]{0:T(128)} %bitcast.bit_ref, f32[2,4,88,128]{3,2,1,0:T(8,128)} %get-tuple-element.14.have_ref, f32[2,4,88,128]{3,2,1,0:T(8,128)} %copy-done.2), custom_call_target="tpu_custom_call" | custom-call | tf_op jit(solution)/shard_map/merge_halves/pallas_call | solution.py:154
  111.1 9.5 %collective-permute-start.3 = (f32[1,4,88,128]{3,2,1,0:T(8,128)}, f32[1,4,88,128]{3,2,1,0:T(8,128)S(1)}, u32[]{:S(2)}, u32[]{:S(2)}) collective-permute-start(f32[1,4,88,128]{3,2,1,0:T(8,128)} %get-tuple-element.17), channel_id=1, source_target_pairs={{0,8},{1,9},{2,10},{3,11},{4,12},{5,13},{6,14},{7,15},{8,0},{9,1},... | collective-permute-start | bytes 540680 | tf_op jit(solution)/shard_map/ppermute | solution.py:293
  121.2 8.2 %collective-permute-done.3.came_ref = f32[1,4,88,128]{3,2,1,0:T(8,128)S(1)} collective-permute-done((f32[1,4,88,128]{3,2,1,0:T(8,128)}, f32[1,4,88,128]{3,2,1,0:T(8,128)S(1)}, u32[]{:S(2)}, u32[]{:S(2)}) %collective-permute-start.3) | collective-permute-done | bytes 180256 | tf_op jit(solution)/shard_map/ppermute | solution.py:293
  130.1 2.1 %final.1 = f32[5,2,32,128]{3,2,1,0:T(8,128)} custom-call(f32[1,4,88,128]{3,2,1,0:T(8,128)} %get-tuple-element.16.have_ref, f32[1,4,88,128]{3,2,1,0:T(8,128)} %copy-done.3, f32[4,88,128]{2,1,0:T(8,128)} %fresh.1.fresh_ref), custom_call_target="tpu_custom_call" | custom-call | tf_op jit(solution)/shard_map/final/pallas_call | solution.py:296
  132.2 5.2 %move_blocks.3 = bf16[32,2,2,16,1024]{4,3,2,1,0:T(8,128)(2,1)} custom-call(s32[32]{0:T(128)} %multiply_add_fusion.1.idx_ref, bf16[32,2,2,16,1024]{4,3,2,1,0:T(8,128)(2,1)} %all-to-all-done.src_ref), custom_call_target="tpu_custom_call" | custom-call | tf_op jit(solution)/shard_map/move_blocks/pallas_call | solution.py:36
  (38 shorter events, 6.6 us)
Async XLA Ops:
  8.3 7.6 %copy-start = (bf16[5,2,4,16384]{3,2,1,0:T(4,128)(2,1)S(1)}, bf16[5,2,4,16384]{3,2,1,0:T(4,128)(2,1)}, u32[]{:S(2)}) copy-start(bf16[5,2,4,16384]{3,2,1,0:T(4,128)(2,1)} %param.11) | copy-start | bytes 3932164
  8.3 123.8 %all-to-all-start = ((bf16[32,2,2,16,1024]{4,3,2,1,0:T(8,128)(2,1)}), bf16[32,2,2,16,1024]{4,3,2,1,0:T(8,128)(2,1)}, u32[]{:S(2)}, u32[]{:S(2)}) async-start(bf16[32,2,2,16,1024]{4,3,2,1,0:T(8,128)(2,1)} %move_blocks.2), calls=%async_computation | async-start | bytes 8388608 | tf_op jit(solution)/shard_map/all_to_all | solution.py:224
  17.3 1.9 %copy-start.5 = (s32[4]{0:T(128)S(1)}, s32[4]{0:T(128)}, u32[]{:S(2)}) copy-start(s32[4]{0:T(128)} %param.10) | copy-start | bytes 52
  54.5 3.6 %collective-permute-start = (f32[8,4,88,128]{3,2,1,0:T(8,128)}, f32[8,4,88,128]{3,2,1,0:T(8,128)}, u32[]{:S(2)}, u32[]{:S(2)}) collective-permute-start(f32[8,4,88,128]{3,2,1,0:T(8,128)} %get-tuple-element.11), channel_id=1, source_target_pairs={{0,1},{1,0},{2,3},{3,2},{4,5},{5,4},{6,7},{7,6},{8,9},{9,8},{10,11... | collective-permute-start | bytes 4325384 | tf_op jit(solution)/shard_map/ppermute | solution.py:293
  58.1 8.9 %copy-start.4 = (s32[512]{0:T(512)S(1)}, s32[512]{0:T(512)}, u32[]{:S(2)}) copy-start(s32[512]{0:T(512)} %param.8) | copy-start | bytes 6148
  64.4 29.5 %collective-permute-start.1 = (f32[4,4,88,128]{3,2,1,0:T(8,128)}, f32[4,4,88,128]{3,2,1,0:T(8,128)S(1)}, u32[]{:S(2)}, u32[]{:S(2)}) collective-permute-start(f32[4,4,88,128]{3,2,1,0:T(8,128)} %get-tuple-element.13), channel_id=1, source_target_pairs={{0,2},{1,3},{2,0},{3,1},{4,6},{5,7},{6,4},{7,5},{8,10},{9,11},{10,... | collective-permute-start | bytes 2162696 | tf_op jit(solution)/shard_map/ppermute | solution.py:293
  93.9 0.9 copy-start.1
  98.6 9.2 %collective-permute-start.2 = (f32[2,4,88,128]{3,2,1,0:T(8,128)}, f32[2,4,88,128]{3,2,1,0:T(8,128)S(1)}, u32[]{:S(2)}, u32[]{:S(2)}) collective-permute-start(f32[2,4,88,128]{3,2,1,0:T(8,128)} %get-tuple-element.15), channel_id=1, source_target_pairs={{0,4},{1,5},{2,6},{3,7},{4,0},{5,1},{6,2},{7,3},{8,12},{9,13},{10,... | collective-permute-start | bytes 1081352 | tf_op jit(solution)/shard_map/ppermute | solution.py:293
  107.7 0.7 copy-start.2
  111.1 18.3 %collective-permute-start.3 = (f32[1,4,88,128]{3,2,1,0:T(8,128)}, f32[1,4,88,128]{3,2,1,0:T(8,128)S(1)}, u32[]{:S(2)}, u32[]{:S(2)}) collective-permute-start(f32[1,4,88,128]{3,2,1,0:T(8,128)} %get-tuple-element.17), channel_id=1, source_target_pairs={{0,8},{1,9},{2,10},{3,11},{4,12},{5,13},{6,14},{7,15},{8,0},{9,1},... | collective-permute-start | bytes 540680 | tf_op jit(solution)/shard_map/ppermute | solution.py:293
  129.4 0.7 copy-start.3
